TPU v7x, 256 devices: a whole 4x4x8 slice. The times are simulated.
256 devices in a mesh: seq: 32 (over x, y, core), head: 8 (over z).
Axes of the slice: x: 4, y: 4, z: 8, core: 2. Of those that a mesh axis runs over, the one named last changes fastest.
Arguments:
- new_states: bfloat16 [96, 1024], replicated, may hold values from -6 to 6
- lengths: int32 [24], replicated, may hold values from 1 to 16380, as said below
- cache_keys: bfloat16 [24, 16384, 1024], P(None, 'seq', 'head'), may hold values from -3000 to 3000
- cache_values: bfloat16 [24, 16384, 1024], P(None, 'seq', 'head'), may hold values from -6 to 6
- buckets: int32 [24, 4, 16384], P(None, None, 'seq'), may hold values from 0 to 31, as said below
- attn_gain: float32 [1024], replicated, may hold values from 0.25 to 1.75
- w_query: bfloat16 [1024, 1024], P(None, 'head'), may hold values from -0.0234375 to 0.0234375
- w_key: bfloat16 [1024, 1024], P(None, 'head'), may hold values from -0.1875 to 0.1875
- w_value: bfloat16 [1024, 1024], P(None, 'head'), may hold values from -0.1875 to 0.1875
- rel_bias: float32 [32, 16], P(None, 'head'), may hold values from -27 to 2
- w_out: bfloat16 [1024, 1024], P('head'), may hold values from -0.1875 to 0.1875
- ffn_gain: float32 [1024], replicated, may hold values from 0.25 to 1.75
- w_router: float32 [1024, 16], replicated, may hold values from -0.1875 to 0.1875
- w_gate: bfloat16 [16, 1024, 2816], P('head', None, 'seq'), may hold values from -0.1875 to 0.1875
- w_up: bfloat16 [16, 1024, 2816], P('head', None, 'seq'), may hold values from -0.1875 to 0.1875
- w_down: bfloat16 [16, 2816, 1024], P('head', 'seq'), may hold values from -0.109375 to 0.109375
- expert_picks: int32 [4, 24, 2], replicated, may hold values from 0 to 15, all different within a row; in each aligned block of 24 rows (0 to 23, 24 to 47, ..., all dimensions but the last counted through in order) at most 4 rows name the same one
- final_gain: float32 [1024], replicated, may hold values from 0.25 to 1.75
- w_vocab: bfloat16 [1024, 32128], P(None, 'seq'), may hold values from -0.5 to 0.5
Outputs:
- final_hidden: bfloat16 [96, 1024], P('head')
- hidden_norm: float32 [96], P('head')
- logit_max: float32 [96], P('head')
Inputs may be any that keep to these rules, and one draw needn't show every extreme that they name: `lengths`: some request has exactly 16380 cached positions. buckets[r, t, p] is the T5 relative position bucket (16 exact buckets, then logarithmic up to a distance of 128) of the distance lengths[r] + t - p where that is not negative, else 0. `expert_picks`: A request's two picks at a step differ; at each step no expert is picked by more than 4 requests, a bound that some block reaches.
All inputs are finite; a program needn't handle non-finite values.
Results may differ from a plain program's by a relative error of at most 0.0096.
Values may be sent and summed in bfloat16 or wider, within the bound.
A program may use at most 64 MiB of HBM per device.

v0:
```python
import jax
import jax.numpy as jnp
from jax import lax
from jax.sharding import PartitionSpec as P

CAP = 4


def joined(part, axis, combine):
    gathered = jax.tree.map(lambda a: lax.all_gather(a, axis), part)

    def take(source):
        return jax.tree.map(lambda a: lax.dynamic_index_in_dim(a, source, 0, False), gathered)

    return lax.fori_loop(
        1, lax.axis_size(axis), lambda source, state: combine(state, take(source)), take(0)
    )


def norm_parts(values, gain_row):
    norm_root = jnp.sqrt(jnp.mean(values * values, axis=-1, keepdims=True) + 1e-06)
    return (values / norm_root * gain_row, norm_root[..., 0])


def join_three(earlier_part, later_part):
    joint_top = jnp.maximum(earlier_part[0], later_part[0])
    lead_scale = jnp.exp(earlier_part[0] - joint_top)
    trail_scale = jnp.exp(later_part[0] - joint_top)
    mass = earlier_part[1] * lead_scale + later_part[1] * trail_scale
    weighted = earlier_part[2] * lead_scale[..., None] + later_part[2] * trail_scale[..., None]
    return (joint_top, mass, weighted)


def shards(
    new_states,
    lengths,
    cache_keys,
    cache_values,
    buckets,
    attn_gain,
    w_query,
    w_key,
    w_value,
    rel_bias,
    w_out,
    ffn_gain,
    w_router,
    w_gate,
    w_up,
    w_down,
    expert_picks,
    final_gain,
    w_vocab,
):
    seq_count = lax.axis_size("seq")
    head_count = lax.axis_size("head")
    seq_index = lax.axis_index("seq")
    head_index = lax.axis_index("head")
    requests, span_local, inner_local = cache_keys.shape
    tokens = new_states.shape[0]
    step_count = tokens // requests
    bucket_count, heads_local = rel_bias.shape
    head_dim = inner_local // heads_local
    states = new_states.astype(jnp.float32)
    scaled, _ = norm_parts(states, attn_gain)
    scaled = scaled.astype(jnp.bfloat16)
    queries = (
        jnp.dot(scaled, w_query, preferred_element_type=jnp.float32)
        .astype(jnp.bfloat16)
        .reshape(requests, step_count, heads_local, head_dim)
    )
    key_new = (
        jnp.dot(scaled, w_key, preferred_element_type=jnp.float32)
        .astype(jnp.bfloat16)
        .reshape(requests, step_count, inner_local)
    )
    value_new = (
        jnp.dot(scaled, w_value, preferred_element_type=jnp.float32)
        .astype(jnp.bfloat16)
        .reshape(requests, step_count, inner_local)
    )
    position = seq_index * span_local + jnp.arange(span_local, dtype=jnp.int32)
    target = lengths[:, None] + jnp.arange(step_count, dtype=jnp.int32)[None, :]
    landing = position[None, None, :] == target[:, :, None]
    landed = jnp.any(landing, axis=1)[:, :, None]
    landing_low = landing.astype(jnp.bfloat16)
    placed_keys = jnp.einsum(
        "rtp,rtc->rpc", landing_low, key_new, preferred_element_type=jnp.float32
    ).astype(jnp.bfloat16)
    placed_values = jnp.einsum(
        "rtp,rtc->rpc", landing_low, value_new, preferred_element_type=jnp.float32
    ).astype(jnp.bfloat16)
    key_rows = jnp.where(landed, placed_keys, cache_keys).reshape(
        requests, span_local, heads_local, head_dim
    )
    value_rows = jnp.where(landed, placed_values, cache_values).reshape(
        requests, span_local, heads_local, head_dim
    )
    scores = jnp.einsum("rthd,rphd->rthp", queries, key_rows, preferred_element_type=jnp.float32)
    bucket_hot = (buckets[..., None] == jnp.arange(bucket_count, dtype=jnp.int32)).astype(
        jnp.float32
    )
    scores = scores + jnp.einsum(
        "rtpb,bh->rthp", bucket_hot, rel_bias, precision=lax.Precision.HIGHEST
    )
    allowed = (position[None, None, :] <= target[:, :, None])[:, :, None, :]
    scores = jnp.where(allowed, scores, -1e30)
    local_top = jnp.max(scores, axis=-1)
    weights = jnp.where(allowed, jnp.exp(scores - local_top[..., None]), 0.0)
    local_mass = jnp.sum(weights, axis=-1)
    partial_value = jnp.einsum(
        "rthp,rphd->rthd", weights, value_rows.astype(jnp.float32), precision=lax.Precision.HIGHEST
    )
    out_rows = w_out.astype(jnp.float32)
    global_top, global_mass, summed = joined(
        (local_top, local_mass, partial_value), "seq", join_three
    )
    heads_out = (summed / global_mass[..., None]).reshape(tokens, inner_local)
    projected = jnp.dot(heads_out, out_rows, precision=lax.Precision.HIGHEST)
    mixed_rows = lax.psum(projected, "head")
    hidden_one = states + mixed_rows
    normed, _ = norm_parts(hidden_one, ffn_gain)
    router_logits = jnp.dot(normed, w_router, precision=lax.Precision.HIGHEST)
    normed_low = normed.astype(jnp.bfloat16)
    expert_total = w_router.shape[1]
    local_experts, model_width, units_local = w_gate.shape
    expert_ids = jnp.arange(expert_total, dtype=jnp.int32)
    pick_marks = (expert_picks[..., None] == expert_ids).astype(jnp.int32)
    per_step = jnp.sum(pick_marks, axis=2)
    earlier = jnp.cumsum(per_step, axis=1) - per_step
    slot_index = jnp.sum(pick_marks * earlier[:, :, None, :], axis=-1)
    pick_total = expert_picks.shape[2]
    token_picks = jnp.transpose(expert_picks, (1, 0, 2)).reshape(tokens, pick_total)
    token_slots = jnp.transpose(slot_index, (1, 0, 2)).reshape(tokens, pick_total)
    token_steps = jnp.arange(tokens, dtype=jnp.int32) % step_count
    picked = jnp.sum(
        jnp.where(token_picks[..., None] == expert_ids, router_logits[:, None, :], 0.0), axis=-1
    )
    gate_first = jax.nn.sigmoid(picked[:, 0] - picked[:, 1])
    gate_second = jax.nn.sigmoid(picked[:, 1] - picked[:, 0])
    slot_rows = step_count * CAP
    row_ids = jnp.arange(local_experts * slot_rows, dtype=jnp.int32)
    row_expert = head_index * local_experts + row_ids // slot_rows
    row_step = row_ids // CAP % step_count
    row_slot = row_ids % CAP
    chooser = jnp.zeros((row_ids.shape[0], tokens), jnp.float32)
    for pick_rank in range(pick_total):
        matched = (
            (row_expert[:, None] == token_picks[None, :, pick_rank])
            & (row_step[:, None] == token_steps[None, :])
            & (row_slot[:, None] == token_slots[None, :, pick_rank])
        )
        chooser = chooser + matched.astype(jnp.float32)
    routed = jnp.dot(
        chooser.astype(jnp.bfloat16), normed_low, preferred_element_type=jnp.float32
    ).astype(jnp.bfloat16)
    routed = routed.reshape(local_experts, slot_rows, model_width)
    gate_part = jnp.einsum("esd,edf->esf", routed, w_gate, preferred_element_type=jnp.float32)
    up_part = jnp.einsum("esd,edf->esf", routed, w_up, preferred_element_type=jnp.float32)
    hidden_units = (jax.nn.gelu(gate_part, approximate=True) * up_part).astype(jnp.bfloat16)
    down_part = jnp.einsum("esf,efd->esd", hidden_units, w_down, preferred_element_type=jnp.float32)
    expert_share = lax.psum_scatter(down_part, "seq", scatter_dimension=2, tiled=True).astype(
        jnp.bfloat16
    )
    share_width = expert_share.shape[2]
    collected = lax.all_gather(expert_share[None], ("seq", "head"), axis=0, tiled=True)
    arranged = collected.reshape(seq_count, head_count, local_experts, slot_rows, share_width)
    arranged = jnp.transpose(arranged, (1, 2, 3, 0, 4)).reshape(
        expert_total * slot_rows, seq_count * share_width
    )
    group_size = tokens // head_count
    first_row = head_index * group_size
    own_picks = lax.dynamic_slice_in_dim(token_picks, first_row, group_size, 0)
    own_slots = lax.dynamic_slice_in_dim(token_slots, first_row, group_size, 0)
    own_steps = lax.dynamic_slice_in_dim(token_steps, first_row, group_size, 0)
    own_first = lax.dynamic_slice_in_dim(gate_first, first_row, group_size, 0)
    own_second = lax.dynamic_slice_in_dim(gate_second, first_row, group_size, 0)
    own_hidden = lax.dynamic_slice_in_dim(hidden_one, first_row, group_size, 0)
    flat_rows = own_picks * slot_rows + own_steps[:, None] * CAP + own_slots
    every_row = jnp.arange(expert_total * slot_rows, dtype=jnp.int32)
    select_first = (flat_rows[:, 0:1] == every_row[None, :]).astype(jnp.bfloat16)
    select_second = (flat_rows[:, 1:2] == every_row[None, :]).astype(jnp.bfloat16)
    expert_mix = own_first[:, None] * jnp.dot(
        select_first, arranged, preferred_element_type=jnp.float32
    )
    expert_mix = expert_mix + own_second[:, None] * jnp.dot(
        select_second, arranged, preferred_element_type=jnp.float32
    )
    final_rows = (own_hidden + expert_mix).astype(jnp.bfloat16)
    scaled_out, norm_root = norm_parts(final_rows.astype(jnp.float32), final_gain)
    logits = jnp.dot(scaled_out.astype(jnp.bfloat16), w_vocab, preferred_element_type=jnp.float32)
    top_logit = lax.pmax(jnp.max(logits, axis=-1), "seq")
    return (final_rows, norm_root, top_logit)


def solution(mesh):
    placed = (
        P(),
        P(),
        P(None, "seq", "head"),
        P(None, "seq", "head"),
        P(None, None, "seq"),
        P(),
        P(None, "head"),
        P(None, "head"),
        P(None, "head"),
        P(None, "head"),
        P("head", None),
        P(),
        P(),
        P("head", None, "seq"),
        P("head", None, "seq"),
        P("head", "seq", None),
        P(),
        P(),
        P(None, "seq"),
    )
    return jax.shard_map(
        shards,
        mesh=mesh,
        in_specs=placed,
        out_specs=(P("head", None), P("head"), P("head")),
        check_vma=False,
    )
```

profile of v0, /device:TPU:1, one launch (start us, length us, event | category | flops | bytes accessed | tf_op | source)
XLA Modules:
  0.0 482.4 jit_solution(6117893066806250847)
XLA Ops:
  7.3 1.2 fusion.13
  8.5 0.7 iota_add_fusion
  9.2 1.3 convolution_convert_fusion.2
  10.7 1.3 convolution_convert_fusion.1
  12.3 4.6 copy.74
  17.0 4.7 copy.77
  22.0 2.0 fusion.4
  24.0 3.1 convert_select_fusion.1
  27.1 1.0 convert_select_fusion
  28.8 3.3 convolution_bitcast_fusion.1
  33.2 26.6 %all-gather.1 = f32[768,4,2]{1,2,0:T(2,128)S(1)} all-gather(f32[24,4,2]{1,2,0:T(2,128)S(1)} %fusion.16), channel_id=3, replica_groups=mesh['seq'=32,'head'=8] {'seq'}, dimensions={0}, use_global_device_ids=true | all-gather | bytes 25344 | tf_op jit(solution)/shard_map/all_gather | solution.py:10
  60.5 25.1 %all-gather = f32[768,4,2]{1,2,0:T(2,128)S(1)} all-gather(f32[24,4,2]{1,2,0:T(2,128)S(1)} %get-tuple-element.240), channel_id=2, replica_groups=mesh['seq'=32,'head'=8] {'seq'}, dimensions={0}, use_global_device_ids=true | all-gather | bytes 25344 | tf_op jit(solution)/shard_map/all_gather | solution.py:10
  85.7 1.2 copy.83
  87.6 0.9 slice.42
  88.5 76.0 %while.19 = (s32[]{:T(128)}, f32[24,4,2]{0,2,1:T(2,128)S(1)}, f32[24,4,2]{0,2,1:T(2,128)S(1)}, f32[24,4,2,64]{3,2,1,0:T(2,128)S(1)}, f32[32,24,4,2]{1,3,2,0:T(2,...) while((s32[]{:T(128)}, f32[24,4,2]{0,2,1:T(2,128)S(1)}, ...), condition=%wide.region_5.6_spmd, body=%wide.region_4.5_spmd.sunk | while | flops 38021 | bytes 256655 | solution.py:15
  89.5 0.9 constant_dynamic-slice_fusion.6
  92.0 0.9 constant_dynamic-slice_fusion.6
  94.4 0.9 constant_dynamic-slice_fusion.6
  96.9 0.9 constant_dynamic-slice_fusion.6
  99.3 0.9 constant_dynamic-slice_fusion.6
  101.8 0.9 constant_dynamic-slice_fusion.6
  103.3 0.7 fusion.99
  104.2 0.9 constant_dynamic-slice_fusion.6
  106.7 0.9 constant_dynamic-slice_fusion.6
  109.1 0.9 constant_dynamic-slice_fusion.6
  111.6 0.9 constant_dynamic-slice_fusion.6
  114.0 0.9 constant_dynamic-slice_fusion.6
  116.5 0.9 constant_dynamic-slice_fusion.6
  118.9 0.9 constant_dynamic-slice_fusion.6
  121.4 0.9 constant_dynamic-slice_fusion.6
  122.9 0.7 fusion.99
  123.9 0.9 constant_dynamic-slice_fusion.6
  126.3 0.9 constant_dynamic-slice_fusion.6
  128.8 0.9 constant_dynamic-slice_fusion.6
  131.2 0.9 constant_dynamic-slice_fusion.6
  133.7 0.9 constant_dynamic-slice_fusion.6
  136.1 0.9 constant_dynamic-slice_fusion.6
  138.5 0.9 constant_dynamic-slice_fusion.6
  140.1 0.7 fusion.99
  141.0 0.9 constant_dynamic-slice_fusion.6
  143.5 0.9 constant_dynamic-slice_fusion.6
  145.9 0.9 constant_dynamic-slice_fusion.6
  148.4 0.9 constant_dynamic-slice_fusion.6
  150.8 0.9 constant_dynamic-slice_fusion.6
  153.3 0.9 constant_dynamic-slice_fusion.6
  155.7 0.9 constant_dynamic-slice_fusion.6
  158.2 0.9 constant_dynamic-slice_fusion.6
  159.7 0.7 fusion.99
  160.6 0.9 constant_dynamic-slice_fusion.6
  163.1 0.9 constant_dynamic-slice_fusion.6
  165.0 1.1 fusion.77
  166.2 67.1 %all-reduce.2.cloned.1.call-done = f32[96,1024]{1,0:T(8,128)} async-done(((f32[96,1024]{1,0:T(8,128)}), f32[96,1024]{1,0:T(8,128)}) %all-reduce.2.cloned.1.call-update) | async-done | bytes 393232 | tf_op jit(solution)/shard_map/psum | solution.py:120
  233.3 1.1 multiply_reduce_fusion
  235.3 1.2 fusion.78
  236.5 2.0 fusion.12
  238.5 1.3 copy.98
  239.8 1.4 reshape.208
  241.4 86.8 %reduce-scatter.4.cloned.1.call-done = f32[32,32]{1,0:T(8,128)} async-done(((f32[1024,32]{1,0:T(8,128)}), f32[32,32]{1,0:T(8,128)}) %reduce-scatter.4.cloned.1.call-update) | async-done | bytes 4112
  328.2 0.8 reshape.209
  329.1 73.7 %all-gather.3 = bf16[512,16,32]{2,1,0:T(8,128)(2,1)S(1)} all-gather(bf16[2,16,32]{2,1,0:T(8,128)(2,1)S(1)} %copy.99), channel_id=5, replica_groups=mesh['seq'=32,'head'=8] {'seq','head'}, dimensions={0}, use_global_device_ids=true | all-gather | bytes 526336 | tf_op jit(solution)/shard_map/all_gather | solution.py:166
  402.8 2.7 copy.112
  405.5 3.5 reshape.189
  409.7 0.8 convolution_reduce_fusion
  410.5 65.4 %pmax.7 = f32[12]{0:T(128)} all-reduce(f32[12]{0:T(128)S(1)} %convolution_reduce_fusion), channel_id=1, replica_groups=mesh['seq'=32,'head'=8] {'seq'}, use_global_device_ids=true, to_apply=%region_15.16 | all-reduce | flops 12 | bytes 96 | tf_op jit(solution)/shard_map/pmax | solution.py:192
  (201 shorter events, 50.7 us)
Async XLA Ops:
  7.2 402.5 %copy-start = (bf16[1024,1004]{0,1:T(8,128)(2,1)S(1)}, bf16[1024,1004]{0,1:T(8,128)(2,1)}, u32[]{:S(2)}) copy-start(bf16[1024,1004]{0,1:T(8,128)(2,1)} %param.39) | copy-start | bytes 6168580
  7.2 4.8 copy-start.2
  7.2 4.8 copy-start.12
  7.2 4.8 copy-start.9
  7.2 80.4 %all-gather.6.cloned.1.call-start = ((), (), s32[]{:S(2)}) async-start(), calls=%async_computation.2 | async-start | bytes 3244032 | tf_op jit(solution)/shard_map/all_gather | solution.py:10
  16.9 5.0 %copy-start.10 = (s32[24,4,512]{2,1,0:T(4,128)S(1)}, s32[24,4,512]{2,1,0:T(4,128)}, u32[]{:S(2)}) copy-start(s32[24,4,512]{2,1,0:T(4,128)} %param.25) | copy-start | bytes 589828
  17.0 5.0 %copy-start.14 = (f32[32,2]{0,1:T(2,128)S(1)}, f32[32,2]{0,1:T(2,128)}, u32[]{:S(2)}) copy-start(f32[32,2]{0,1:T(2,128)} %param.30) | copy-start | bytes 772
  24.0 3.1 copy-start.1
  28.8 3.3 copy-start.6
  32.1 201.2 %all-reduce.2.cloned.1.call-start = ((), (), s32[]{:S(2)}) async-start(), calls=%async_computation.1 | async-start | bytes 786432 | tf_op jit(solution)/shard_map/psum | solution.py:120
  60.4 104.6 %copy-start.4 = (bf16[128,1024]{1,0:T(8,128)(2,1)S(1)}, bf16[128,1024]{1,0:T(8,128)(2,1)}, u32[]{:S(2)}) copy-start(bf16[128,1024]{1,0:T(8,128)(2,1)} %param.31) | copy-start | bytes 786436
  88.5 145.9 %copy-start.11 = (f32[1024,16]{0,1:T(8,128)S(1)}, f32[1024,16]{0,1:T(8,128)}, u32[]{:S(2)}) copy-start(f32[1024,16]{0,1:T(8,128)} %param.33) | copy-start | bytes 196612
  88.5 145.9 %copy-start.13 = (f32[1024]{0:T(1024)S(1)}, f32[1024]{0:T(1024)}, u32[]{:S(2)}) copy-start(f32[1024]{0:T(1024)} %param.32) | copy-start | bytes 12292
  164.6 71.9 %copy-start.3 = (bf16[2,88,1024]{2,1,0:T(8,128)(2,1)S(1)}, bf16[2,88,1024]{2,1,0:T(8,128)(2,1)}, u32[]{:S(2)}) copy-start(bf16[2,88,1024]{2,1,0:T(8,128)(2,1)} %param.36) | copy-start | bytes 1081348
  166.1 162.1 %reduce-scatter.4.cloned.1.call-start = ((), (), s32[]{:S(2)}) async-start(), calls=%async_computation.3 | async-start | bytes 540672
  402.8 6.9 %copy-start.7 = (f32[1024]{0:T(1024)S(1)}, f32[1024]{0:T(1024)}, u32[]{:S(2)}) copy-start(f32[1024]{0:T(1024)} %param.38) | copy-start | bytes 12292
  409.6 66.2 %copy-start.5 = (bf16[12,1024]{1,0:T(8,128)(2,1)}, bf16[12,1024]{1,0:T(8,128)(2,1)S(1)}, u32[]{:S(2)}) copy-start(bf16[12,1024]{1,0:T(8,128)(2,1)S(1)} %get-tuple-element.243) | copy-start | bytes 73732
  409.7 66.2 %copy-start.8 = (f32[12]{0:T(128)}, f32[12]{0:T(128)S(1)}, u32[]{:S(2)}) copy-start(f32[12]{0:T(128)S(1)} %add_sqrt_fusion) | copy-start | bytes 148
Sparse Core Ops, SparseCore 0:
  32.2 55.3 all-gather.5
  166.2 67.0 all-reduce.1
  241.4 86.8 reduce-scatter.3
where the time goes:
time: 485 us; the launch traced here: 482 us
  blocking collectives  191 us (39%)
  waiting for transfers between devices  155 us (32%)
  local copies, waits for them, and re-layouts  58.1 us (12%)
  other arithmetic  44.9 us (9%)
  matrix products  19.3 us (4%)
  between operations  14.1 us (3%)
    unnamed x4, waiting for transfers between devices  86.9 us
    all_gather x1, blocking collectives, shards(): lax.all_gather(expert_share[None], ('seq', 'head'), axis=0, tiled=True)  73.7 us
    psum x1, waiting for transfers between devices, shards(): mixed_rows = lax.psum(projected, 'head')  67.1 us
    pmax x1, blocking collectives, shards(): top_logit = lax.pmax(jnp.max(logits, axis=-1), 'seq')  65.4 us
    all_gather x2, blocking collectives, joined(): gathered = jax.tree.map(lambda a: lax.all_gather(a, axis), part)  51.7 us
    dynamic_slice x34, local copies, waits for them, and re-layouts, take(): lax.dynamic_index_in_dim(a, source, 0, False)  28.9 us
    add x31, other arithmetic, join_three(): mass = earlier_part[1] * lead_scale + later_part[1] * trail_scale  21.9 us
    add x31, other arithmetic, join_three(): earlier_part[2] * lead_scale[..., None]  18.8 us
  transfers between devices with their start and end apart: 3, of which 3 were waited for; matrix products, arithmetic and copies ran while one was open for 1% of the time, Pallas kernels for 0%

commit v1 on v0

v1 whole, which is shorter than its diff:
```python
import functools

import jax
import jax.numpy as jnp
from jax import lax
from jax.experimental import pallas as pl
from jax.experimental.pallas import tpu as pltpu
from jax.sharding import PartitionSpec as P

F32 = jnp.float32
BF16 = jnp.bfloat16
CAP = 4
EPS = 1e-06
LOW = -1e30
MESH = pl.DeviceIdType.MESH
NT = (((1,), (1,)), ((), ()))
HIGH = lax.Precision.HIGHEST


def iota(shape, dim):
    return lax.broadcasted_iota(jnp.int32, shape, dim)


def dot(a, b):
    return jnp.dot(a, b, preferred_element_type=F32)


def dot_nt(a, b, precision=None):
    return lax.dot_general(a, b, NT, precision=precision, preferred_element_type=F32)


def local_kernel(
    per,
    len_ref,
    x_ref,
    ag_ref,
    wq_ref,
    wk_ref,
    wv_ref,
    rb_ref,
    pk_ref,
    k_ref,
    v_ref,
    b_ref,
    a_ref,
    chl_ref,
    chr_ref,
    cbl_ref,
    cbr_ref,
    eo_ref,
    q_sc,
    kn_sc,
    vn_sc,
    tb_sc,
):
    step = pl.program_id(0)
    seq = lax.axis_index("seq")
    head = lax.axis_index("head")
    row = iota((8, 128), 0)
    lane = iota((8, 128), 1)
    own = (lane < 64) == (row < 4)

    @pl.when(step == 0)
    def _():
        x = x_ref[...].astype(F32)
        root = jnp.sqrt(jnp.mean(x * x, axis=-1, keepdims=True) + EPS)
        scaled = (x / root * ag_ref[...]).astype(BF16)
        i, j = iota((192, 96), 0), iota((192, 96), 1)
        spread = jnp.where(j == (i // 8) * 4 + i % 4, 1.0, 0.0).astype(BF16)
        keep = (iota((192, 128), 1) < 64) == (iota((192, 128), 0) % 8 < 4)
        q = dot(spread, dot(scaled, wq_ref[...]).astype(BF16))
        q_sc[...] = jnp.where(keep, q, 0.0).reshape(24, 8, 128)
        kn_sc[...] = dot(spread, dot(scaled, wk_ref[...]).astype(BF16)).reshape(24, 8, 128)
        v = dot(spread, dot(scaled, wv_ref[...]).astype(BF16))
        v = jnp.where(iota((192, 128), 0) % 8 < 4, v, 0.0)
        vn_sc[...] = v.reshape(24, 8, 128)
        tb_sc[...] = jnp.zeros((8, 128), F32)
        tb_sc[:, 0:32] = jnp.where(iota((8, 32), 0) < 4, rb_ref[0:1, :], rb_ref[1:2, :])
        i = iota((32, 24), 0)
        e, t, c = head * 2 + i // 16, (i // 4) % 4, i % 4
        p0 = jnp.zeros((32, 24), jnp.int32)
        p1 = jnp.zeros((32, 24), jnp.int32)
        for s in range(4):
            p0 = jnp.where(t == s, pk_ref[s : s + 1, :], p0)
            p1 = jnp.where(t == s, pk_ref[4 + s : 5 + s, :], p1)
        inc = jnp.where((p0 == e) | (p1 == e), 1.0, 0.0)
        upper = jnp.where(iota((24, 24), 0) < iota((24, 24), 1), 1.0, 0.0)
        before = dot(inc.astype(BF16), upper.astype(BF16))
        ch = jnp.where(before == c.astype(F32), inc, 0.0)
        other = jnp.sum(ch * (p0 + p1 - e).astype(F32), axis=1, keepdims=True)
        n = iota((32, 16), 1)
        e16 = head * 2 + iota((32, 16), 0) // 16
        eo_ref[...] = jnp.where(n == e16, 1.0, 0.0) - jnp.where(n.astype(F32) == other, 1.0, 0.0)
        ch = ch.astype(BF16)
        grow = jnp.where(iota((24, 192), 1) // 8 == iota((24, 192), 0), 1.0, 0.0).astype(BF16)
        wide = dot(ch, grow)
        l8, t_r = iota((32, 192), 1) % 8, (iota((32, 192), 0) // 4) % 4
        chl_ref[...] = jnp.where(l8 == t_r, wide, 0.0).astype(BF16)
        chr_ref[...] = jnp.where(l8 == t_r + 4, wide, 0.0).astype(BF16)
        grow_t = jnp.where(iota((192, 24), 0) // 8 == iota((192, 24), 1), 1.0, 0.0).astype(BF16)
        tall = dot_nt(grow_t, ch)
        r8, t_l = iota((192, 32), 0) % 8, (iota((192, 32), 1) // 4) % 4
        cbl_ref[...] = jnp.where(r8 == t_l, tall, 0.0).astype(BF16)
        cbr_ref[...] = jnp.where(r8 == t_l + 4, tall, 0.0).astype(BF16)

    span = k_ref.shape[1]
    wide_row = iota((8, span), 0)
    wide_pos = iota((8, span), 1) + seq * span
    table = tb_sc[...]
    for i in range(per):
        r = step * per + i
        rel = wide_pos - len_ref[r]
        q8 = q_sc[r].astype(BF16)
        scores = dot_nt(q8, k_ref[i])
        fresh = dot_nt(q8, kn_sc[r].astype(BF16))
        for t in range(4):
            scores = jnp.where(rel == t, fresh[:, t : t + 1], scores)
        b4 = b_ref[i]
        b8 = jnp.concatenate([b4, b4], axis=0)
        bias = jnp.concatenate(
            [
                jnp.take_along_axis(
                    table, b8[:, c * 128 : c * 128 + 128], axis=1, mode="promise_in_bounds"
                )
                for c in range(span // 128)
            ],
            axis=1,
        )
        allowed = rel <= wide_row % 4
        scores = jnp.where(allowed, scores + bias, LOW)
        top = jnp.max(scores, axis=1, keepdims=True)
        weights = jnp.where(allowed, jnp.exp(scores - top), 0.0)
        mass = jnp.sum(weights, axis=1, keepdims=True)
        landed = (rel >= 0) & (rel < 4)
        hot = jnp.where(rel == wide_row, 1.0, 0.0).astype(BF16)
        summed = dot(jnp.where(landed, 0.0, weights).astype(BF16), v_ref[i])
        w_new = dot_nt(weights.astype(BF16), hot)
        summed = summed + dot(w_new.astype(BF16), vn_sc[r].astype(BF16))
        a_ref[i] = jnp.where(own, summed, jnp.where(lane % 64 < 32, top, mass))


def exchange_kernel(
    a_ref,
    x_ref,
    wo_ref,
    fg_ref,
    wr_ref,
    chl_ref,
    chr_ref,
    cbl_ref,
    cbr_ref,
    eo_ref,
    og_ref,
    wg_hbm,
    wu_hbm,
    wd_hbm,
    wv_hbm,
    fin_ref,
    stat_ref,
    wg,
    wu,
    wd,
    wv,
    in1,
    out2,
    in2,
    out3,
    in3,
    out4,
    in4,
    out5,
    in5,
    out6,
    in6,
    out7,
    in7,
    hid,
    load_sem,
    send_sem,
    recv_sem,
    fin_sem,
):
    seq_count, head_count = 32, 8
    me = lax.axis_index("seq")
    z = lax.axis_index("head")
    owner = me % 4 != 3
    mine = (me // 4) * 3 + me % 4
    home = me // 4

    loads = [
        pltpu.make_async_copy(src, dst, load_sem.at[n])
        for n, (src, dst) in enumerate(((wg_hbm, wg), (wu_hbm, wu), (wd_hbm, wd), (wv_hbm, wv)))
    ]
    for load in loads:
        load.start()

    barrier = pltpu.get_barrier_semaphore()

    @pl.loop(1, seq_count)
    def _(n):
        pl.semaphore_signal(
            barrier, inc=1, device_id={"seq": (me + n) % seq_count}, device_id_type=MESH
        )

    @pl.loop(1, head_count)
    def _(n):
        pl.semaphore_signal(
            barrier, inc=1, device_id={"head": (z + n) % head_count}, device_id_type=MESH
        )

    pl.semaphore_wait(barrier, seq_count + head_count - 2)

    def send(stage, src, dst, target, sem=None):
        pltpu.make_async_remote_copy(
            src_ref=src,
            dst_ref=dst,
            send_sem=send_sem.at[stage],
            recv_sem=recv_sem.at[stage] if sem is None else sem,
            device_id=target,
            device_id_type=MESH,
        ).start()

    def await_bytes(ref, sem):
        pltpu.make_async_copy(ref, ref, sem).wait()

    row = iota((8, 512), 0)
    upper = row < 4

    def fold(rows):
        return jnp.where(upper, rows[:, :512], rows[:, 512:])

    def pair_mean(values):
        total = jnp.sum(values * values, axis=1, keepdims=True)
        return (total + jnp.concatenate([total[4:8], total[0:4]], axis=0)) / 1024.0

    @pl.loop(1, seq_count)
    def _(n):
        target = (me + n) % seq_count

        @pl.when(target % 4 != 3)
        def _():
            request = (target // 4) * 3 + target % 4
            send(0, a_ref.at[request], in1.at[n], {"seq": target})

    @pl.when(owner)
    def _():
        in1[0] = a_ref[mine]
        i, j = iota((8, 96), 0), iota((8, 96), 1)
        pick = jnp.where(j == mine * 4 + i % 4, 1.0, 0.0).astype(BF16)
        states = fold(dot(pick, x_ref[...]))
        await_bytes(in1.at[pl.ds(0, 31)], recv_sem.at[0])
        part = in1[...]
        r3, l3 = iota((32, 8, 128), 1), iota((32, 8, 128), 2)
        spare = (l3 < 64) != (r3 < 4)
        tops = jnp.max(
            jnp.where(spare & (l3 % 64 < 32), part, -3e38), axis=2, keepdims=True
        )
        masses = jnp.max(
            jnp.where(spare & (l3 % 64 >= 32), part, -3e38), axis=2, keepdims=True
        )
        lead = jnp.exp(tops - jnp.max(tops, axis=0, keepdims=True))
        mass = jnp.sum(masses * lead, axis=0)
        both = jnp.sum(part * lead, axis=0) / mass
        swapped = jnp.concatenate([both[4:8], both[0:4]], axis=0)
        mixed = jnp.where((iota((8, 128), 1) < 64) == (iota((8, 128), 0) < 4), both, swapped)
        coarse = mixed.astype(BF16)
        fine = (mixed - coarse.astype(F32)).astype(BF16)
        wo = wo_ref[...]
        term = fold(dot(coarse, wo) + dot(fine, wo)).astype(BF16)
        out2[...] = term
        in2[z] = term

        @pl.loop(1, head_count)
        def _(n):
            send(1, out2, in2.at[z], {"head": (z + n) % head_count})

        await_bytes(in2.at[pl.ds(0, 7)], recv_sem.at[1])
        hidden = states + jnp.sum(in2[...].astype(F32), axis=0)
        hid[...] = hidden
        gain = jnp.where(upper, fg_ref[:, :512], fg_ref[:, 512:])
        normed = (hidden / jnp.sqrt(pair_mean(hidden) + EPS) * gain).astype(BF16)
        out3[...] = normed
        in3[mine] = normed

        @pl.loop(1, seq_count)
        def _(n):
            send(2, out3, in3.at[mine], {"seq": (me + n) % seq_count})

        await_bytes(in3.at[pl.ds(0, 23)], recv_sem.at[2])

    @pl.when(me % 4 == 3)
    def _():
        await_bytes(in3, recv_sem.at[2])

    rows = in3[...].astype(F32).reshape(192, 512).astype(BF16)
    routed = jnp.concatenate([dot(chl_ref[...], rows), dot(chr_ref[...], rows)], axis=1)
    logits = dot_nt(routed, wr_ref[...], HIGH)
    delta = jnp.sum(logits * eo_ref[...], axis=1, keepdims=True)
    gate = 1.0 / (1.0 + jnp.exp(-delta))
    routed = routed.astype(BF16)
    for load in loads[:3]:
        load.wait()
    downs = []
    for e in range(2):
        slots = routed[e * 16 : e * 16 + 16]
        gated = jax.nn.gelu(dot_nt(slots, wg[e]), approximate=True)
        units = (gated * dot_nt(slots, wu[e])).astype(BF16)
        downs.append(dot(units, wd[e]))
    down = (jnp.concatenate(downs, axis=0) * gate).astype(BF16)
    spread = dot(cbl_ref[...], down[:, :512]) + dot(cbr_ref[...], down[:, 512:])
    out4[...] = spread.reshape(24, 8, 512).astype(BF16)

    @pl.loop(1, seq_count)
    def _(n):
        target = (me + n) % seq_count

        @pl.when(target % 4 != 3)
        def _():
            request = (target // 4) * 3 + target % 4
            send(3, out4.at[request], in4.at[n], {"seq": target})

    @pl.when(owner)
    def _():
        in4[0] = out4[mine]
        await_bytes(in4.at[pl.ds(0, 31)], recv_sem.at[3])
        mix = jnp.sum(in4[...].astype(F32), axis=0)

        @pl.when(z != home)
        def _():
            out5[...] = mix.astype(BF16)
            send(4, out5, in5.at[z], {"head": home})

        @pl.when(z == home)
        def _():
            in5[z] = mix.astype(BF16)
            await_bytes(in5.at[pl.ds(0, 7)], recv_sem.at[4])
            final = (hid[...] + jnp.sum(in5[...].astype(F32), axis=0)).astype(BF16)
            out6[...] = final
            in6[me % 4] = final

            @pl.loop(1, seq_count)
            def _(n):
                send(
                    5,
                    out6,
                    in6.at[me % 4],
                    {"seq": (me + n) % seq_count},
                    fin_sem.at[me % 4],
                )

    for k in range(3):

        @pl.when(me != z * 4 + k)
        def _():
            await_bytes(in6.at[k], fin_sem.at[k])

    rows = in6[...].astype(F32)
    total = jnp.sum(rows * rows, axis=2, keepdims=True)
    total = total + jnp.concatenate([total[:, 4:8], total[:, 0:4]], axis=1)
    root = jnp.sqrt(total / 1024.0 + EPS)
    gain = jnp.where(upper, og_ref[:, :512], og_ref[:, 512:])
    scaled = (rows / root * gain[None]).reshape(24, 512).astype(BF16)
    loads[3].wait()
    left = dot_nt(scaled, wv[:, :512])
    right = dot_nt(scaled, wv[:, 512:])
    width = wv.shape[0]
    left = left.reshape(3, 8, width)[:, 0:4]
    right = right.reshape(3, 8, width)[:, 4:8]
    best = jnp.max(left + right, axis=2, keepdims=True)
    token = iota((3, 4, 128), 0) * 4 + iota((3, 4, 128), 1)
    place = iota((3, 4, 128), 2) == token
    best = jnp.sum(jnp.sum(jnp.where(place, best, 0.0), axis=0), axis=0, keepdims=True)
    roots = jnp.sum(jnp.sum(jnp.where(place, root[:, 0:4], 0.0), axis=0), axis=0, keepdims=True)
    best = jnp.broadcast_to(best, (8, 128))
    out7[...] = best
    in7[0] = best

    @pl.loop(1, seq_count)
    def _(n):
        send(6, out7, in7.at[n], {"seq": (me + n) % seq_count})

    halves = [jnp.concatenate([rows[k, 0:4], rows[k, 4:8]], axis=1) for k in range(3)]
    fin_ref[...] = jnp.concatenate(halves, axis=0).astype(BF16)
    await_bytes(in7.at[pl.ds(0, 31)], recv_sem.at[6])
    best = jnp.max(in7[...], axis=0)
    stat_ref[...] = jnp.where(iota((8, 128), 0) == 0, roots, best)

    @pl.when(owner)
    def _():
        await_bytes(a_ref.at[pl.ds(0, 23)], send_sem.at[0])
        await_bytes(in2.at[pl.ds(0, 7)], send_sem.at[1])
        await_bytes(in4.at[pl.ds(0, 31)], send_sem.at[2])
        await_bytes(out4.at[pl.ds(0, 23)], send_sem.at[3])

        @pl.when(z != home)
        def _():
            await_bytes(out5, send_sem.at[4])

        @pl.when(z == home)
        def _():
            await_bytes(in4.at[pl.ds(0, 31)], send_sem.at[5])

    @pl.when(me % 4 == 3)
    def _():
        await_bytes(a_ref, send_sem.at[0])
        await_bytes(out4, send_sem.at[3])

    await_bytes(in7.at[pl.ds(0, 31)], send_sem.at[6])


def shards(
    new_states,
    lengths,
    cache_keys,
    cache_values,
    buckets,
    attn_gain,
    w_query,
    w_key,
    w_value,
    rel_bias,
    w_out,
    ffn_gain,
    w_router,
    w_gate,
    w_up,
    w_down,
    expert_picks,
    final_gain,
    w_vocab,
):
    requests, span, inner = cache_keys.shape
    per = 6
    whole = pl.BlockSpec(memory_space=pltpu.VMEM)
    smem = pl.BlockSpec(memory_space=pltpu.SMEM)
    anywhere = pl.BlockSpec(memory_space=pl.ANY)
    picks = jnp.transpose(expert_picks, (2, 0, 1)).reshape(8, requests)

    def fixed(shape):
        return pl.BlockSpec(shape, lambda i: (0,) * len(shape))

    shapes = [(32, 192), (32, 192), (192, 32), (192, 32), (32, 16)]
    types = [BF16, BF16, BF16, BF16, F32]
    tables = pl.pallas_call(
        functools.partial(local_kernel, per),
        grid=(requests // per,),
        out_shape=[jax.ShapeDtypeStruct((requests, 8, 128), F32)]
        + [jax.ShapeDtypeStruct(s, t) for s, t in zip(shapes, types)],
        in_specs=[smem]
        + [fixed(s) for s in ((96, 1024), (1, 1024), (1024, 128), (1024, 128), (1024, 128), (2, 32), (8, 24))]
        + [
            pl.BlockSpec((per, span, inner), lambda i: (i, 0, 0)),
            pl.BlockSpec((per, span, inner), lambda i: (i, 0, 0)),
            pl.BlockSpec((per, 4, span), lambda i: (i, 0, 0)),
        ],
        out_specs=[pl.BlockSpec((per, 8, 128), lambda i: (i, 0, 0))] + [fixed(s) for s in shapes],
        scratch_shapes=[pltpu.VMEM((24, 8, 128), F32)] * 3 + [pltpu.VMEM((8, 128), F32)],
        name="local_attention",
    )(
        lengths,
        new_states,
        attn_gain[None],
        w_query,
        w_key,
        w_value,
        rel_bias.T,
        picks,
        cache_keys,
        cache_values,
        buckets,
    )
    partial, rest = tables[0], tables[1:]
    vocab = w_vocab.T
    final, stats = pl.pallas_call(
        exchange_kernel,
        out_shape=(
            jax.ShapeDtypeStruct((12, 1024), BF16),
            jax.ShapeDtypeStruct((8, 128), F32),
        ),
        in_specs=[whole] * 11 + [anywhere] * 4,
        out_specs=(whole, whole),
        scratch_shapes=[
            pltpu.VMEM((2, 88, 1024), BF16),
            pltpu.VMEM((2, 88, 1024), BF16),
            pltpu.VMEM((2, 88, 1024), BF16),
            pltpu.VMEM(vocab.shape, BF16),
            pltpu.VMEM((32, 8, 128), F32),
            pltpu.VMEM((8, 512), BF16),
            pltpu.VMEM((8, 8, 512), BF16),
            pltpu.VMEM((8, 512), BF16),
            pltpu.VMEM((24, 8, 512), BF16),
            pltpu.VMEM((24, 8, 512), BF16),
            pltpu.VMEM((32, 8, 512), BF16),
            pltpu.VMEM((8, 512), BF16),
            pltpu.VMEM((8, 8, 512), BF16),
            pltpu.VMEM((8, 512), BF16),
            pltpu.VMEM((3, 8, 512), BF16),
            pltpu.VMEM((8, 128), F32),
            pltpu.VMEM((32, 8, 128), F32),
            pltpu.VMEM((8, 512), F32),
            pltpu.SemaphoreType.DMA((4,)),
            pltpu.SemaphoreType.DMA((7,)),
            pltpu.SemaphoreType.DMA((7,)),
            pltpu.SemaphoreType.DMA((3,)),
        ],
        compiler_params=pltpu.CompilerParams(collective_id=0, has_side_effects=True),
        name="exchange",
    )(
        partial,
        new_states,
        w_out,
        ffn_gain[None],
        w_router.T,
        *rest,
        final_gain[None],
        jnp.transpose(w_gate, (0, 2, 1)),
        jnp.transpose(w_up, (0, 2, 1)),
        w_down,
        vocab,
    )
    return final, stats[0, :12], stats[1, :12]


def solution(mesh):
    placed = (
        P(),
        P(),
        P(None, "seq", "head"),
        P(None, "seq", "head"),
        P(None, None, "seq"),
        P(),
        P(None, "head"),
        P(None, "head"),
        P(None, "head"),
        P(None, "head"),
        P("head", None),
        P(),
        P(),
        P("head", None, "seq"),
        P("head", None, "seq"),
        P("head", "seq", None),
        P(),
        P(),
        P(None, "seq"),
    )
    return jax.shard_map(
        shards,
        mesh=mesh,
        in_specs=placed,
        out_specs=(P("head", None), P("head"), P("head")),
        check_vma=False,
    )
```

time: 485 us -> 73.7 us (0.15)
  blocking collectives: 191 us -> 0 us
  waiting for transfers between devices: 155 us -> 0 us
  Pallas kernels: 0 us -> 68.9 us
  local copies, waits for them, and re-layouts: 58.1 us -> 3.93 us
  other arithmetic: 44.9 us -> 0 us
  matrix products: 19.3 us -> 0 us
  between operations: 14.1 us -> 0.64 us
    all_gather x3 -> x0, blocking collectives: 125 us -> none  [the longest x1 73.7 us: shards(): lax.all_gather(expert_share[None], ('seq', 'head'), axis=0, tiled=True)]
    unnamed x4 -> x0, waiting for transfers between devices: 86.9 us -> none
    pallas_call x0 -> x2, Pallas kernels: none -> 68.9 us  [the longest x1 53.7 us: shards(): pl.pallas_call(exchange_kernel, out_shape=(jax.ShapeDtypeStruct((12, 1024...]
    psum x1 -> x0, waiting for transfers between devices: 67.1 us -> none  [shards(): mixed_rows = lax.psum(projected, 'head')]
    pmax x1 -> x0, blocking collectives: 65.4 us -> none  [shards(): top_logit = lax.pmax(jnp.max(logits, axis=-1), 'seq')]
    add x66 -> x0, other arithmetic: 41.5 us -> none  [the longest x31 21.9 us: join_three(): mass = earlier_part[1] * lead_scale + later_part[1] * trail_scale]
    dynamic_slice x36 -> x0, local copies, waits for them, and re-layouts: 29 us -> none  [the longest x34 28.9 us: take(): lax.dynamic_index_in_dim(a, source, 0, False)]
    dot_general x16 -> x0, matrix products: 19.3 us -> none  [the longest x1 3.26 us: shards(): jnp.einsum('rthp,rphd->rthd', weights, value_rows.astype(jnp.float32), pr...]
  transfers between devices with their start and end apart: 3 -> 0, of which waited for: 3 -> 0; matrix products, arithmetic and copies ran while one was open for 1% -> 0% of each run, Pallas kernels for 0% -> 0%
where the time goes in v1:
time: 73.7 us; the launch traced here: 73.4 us
  Pallas kernels  68.9 us (93%)
  local copies, waits for them, and re-layouts  3.93 us (5%)
    pallas_call x1, Pallas kernels, shards(): pl.pallas_call(exchange_kernel, out_shape=(jax.ShapeDtypeStruct((12, 1024...  53.7 us
    pallas_call x1, Pallas kernels, shards(): pl.pallas_call(functools.partial(local_kernel, per), grid=(requests // pe...  15.2 us

profile of v1, /device:TPU:1, one launch (start us, length us, event | category | flops | bytes accessed | tf_op | source)
XLA Modules:
  0.0 73.4 jit_solution(6554207779470555522)
XLA Ops:
  0.6 1.3 %copy.22 = s32[2,4,24]{2,1,0:T(4,128)} copy(s32[2,4,24]{2,0,1:T(2,128)} %bitcast.20) | data formatting | bytes 1536 | tf_op jit(solution)/shard_map/transpose | solution.py:437
  1.9 15.2 %local_attention.1 = (f32[24,8,128]{2,1,0:T(8,128)}, bf16[32,192]{1,0:T(8,128)(2,1)}, bf16[32,192]{1,0:T(8,128)(2,1)}, bf16[192,32]{1,0:T(8,128)(2,1)}, bf16[192,32]{1,0:T(8,128)(2,1)}, /*index=5*/f32[32,16]{1,0:T(8,128)}) custom-call(s32[24]{0:T(128)} %len_ref.1, bf16[96,1024]{1,0:T(8,128)(2,1)} %x_ref.3, f32[1,1024]{1,0:T(1,128)} %bitcast.19, ...), custom_call_target="tpu_custom_call" | custom-call | tf_op jit(solution)/shard_map/local_attention/pallas_call | solution.py:444
  17.1 53.7 %exchange.1 = (bf16[12,1024]{1,0:T(8,128)(2,1)}, f32[8,128]{1,0:T(8,128)}) custom-call(f32[24,8,128]{2,1,0:T(8,128)} %get-tuple-element.11.a_ref, bf16[96,1024]{1,0:T(8,128)(2,1)} %x_ref.3, bf16[128,1024]{1,0:T(8,128)(2,1)} %wo_ref.1, f32[1,1024]{1,0:T(1,128)} %bitcast.21, f32[16,1024]{1,0:T(8,128)} %bitcast.17, bf16[32,192]{1,0:T(8,128)(2,1)} %get-tuple-element.12.chl_ref, ...), custom_call_target="tpu_custom_call" | custom-call | tf_op jit(solution)/shard_map/exchange/pallas_call | solution.py:474
  70.8 1.3 %slice_bitcast_fusion = (f32[12]{0:T(128)}, f32[12]{0:T(128)}) fusion(f32[8,128]{1,0:T(8,128)} %get-tuple-element.18), kind=kLoop, calls=%fused_computation | loop fusion | bytes 192 | tf_op jit(solution)/shard_map/squeeze | solution.py:521
  72.0 1.4 %copy.24 = bf16[12,1024]{1,0:T(8,128)(2,1)} copy(bf16[12,1024]{1,0:T(8,128)(2,1)} %get-tuple-element.24) | data formatting | bytes 49152

commit v2 on v1

v2 whole, which is shorter than its diff:
```python
import functools

import jax
import jax.numpy as jnp
from jax import lax
from jax.experimental import pallas as pl
from jax.experimental.pallas import tpu as pltpu
from jax.sharding import PartitionSpec as P

F32 = jnp.float32
BF16 = jnp.bfloat16
CAP = 4
EPS = 1e-06
LOW = -1e30
MESH = pl.DeviceIdType.MESH
NT = (((1,), (1,)), ((), ()))
HIGH = lax.Precision.HIGHEST


def iota(shape, dim):
    return lax.broadcasted_iota(jnp.int32, shape, dim)


def dot(a, b):
    return jnp.dot(a, b, preferred_element_type=F32)


def dot_nt(a, b, precision=None):
    return lax.dot_general(a, b, NT, precision=precision, preferred_element_type=F32)


def layer_kernel(
    per,
    len_ref,
    ag_ref,
    rb_ref,
    pk_ref,
    fg_ref,
    wr_ref,
    og_ref,
    x_hbm,
    wq_hbm,
    wk_hbm,
    wv_hbm,
    k_hbm,
    v_hbm,
    b_hbm,
    wo_hbm,
    wg_hbm,
    wu_hbm,
    wd_hbm,
    voc_hbm,
    fin_ref,
    stat_ref,
    xb,
    wq,
    wk,
    wv,
    kb,
    vb,
    bb,
    wo,
    wg,
    wu,
    wd,
    voc,
    q_sc,
    kn_sc,
    vn_sc,
    tb_sc,
    chl_sc,
    chr_sc,
    cbl_sc,
    cbr_sc,
    eo_sc,
    wr_sc,
    part_sc,
    in1,
    out2,
    in2,
    out3,
    in3,
    out4,
    in4,
    out5,
    in5,
    out6,
    in6,
    out7,
    in7,
    hid,
    load_sem,
    k_sem,
    v_sem,
    send_sem,
    recv_sem,
    fin_sem,
):
    seq_count, head_count = 32, 8
    me = lax.axis_index("seq")
    z = lax.axis_index("head")
    owner = me % 4 != 3
    mine = (me // 4) * 3 + me % 4
    home = me // 4
    requests, span = kb.shape[0], kb.shape[1]
    chunks = requests // per

    def cache_load(src, dst, sem, c):
        rows = pl.ds(c * per, per)
        return pltpu.make_async_copy(src.at[rows], dst.at[rows], sem.at[c])

    first = [(x_hbm, xb), (wq_hbm, wq), (wk_hbm, wk), (wv_hbm, wv), (b_hbm, bb)]
    later = [(wo_hbm, wo), (wg_hbm, wg), (wu_hbm, wu), (wd_hbm, wd), (voc_hbm, voc)]
    loads = [
        pltpu.make_async_copy(src, dst, load_sem.at[n]) for n, (src, dst) in enumerate(first + later)
    ]
    for load in loads[:5]:
        load.start()
    for c in range(chunks):
        cache_load(k_hbm, kb, k_sem, c).start()
        cache_load(v_hbm, vb, v_sem, c).start()
    for load in loads[5:]:
        load.start()

    barrier = pltpu.get_barrier_semaphore()

    @pl.loop(1, seq_count)
    def _(n):
        pl.semaphore_signal(
            barrier, inc=1, device_id={"seq": (me + n) % seq_count}, device_id_type=MESH
        )

    @pl.loop(1, head_count)
    def _(n):
        pl.semaphore_signal(
            barrier, inc=1, device_id={"head": (z + n) % head_count}, device_id_type=MESH
        )

    def send(stage, src, dst, target, sem=None):
        pltpu.make_async_remote_copy(
            src_ref=src,
            dst_ref=dst,
            send_sem=send_sem.at[stage],
            recv_sem=recv_sem.at[stage] if sem is None else sem,
            device_id=target,
            device_id_type=MESH,
        ).start()

    def await_bytes(ref, sem):
        pltpu.make_async_copy(ref, ref, sem).wait()

    i = iota((32, 24), 0)
    e, t, c = z * 2 + i // 16, (i // 4) % 4, i % 4
    p0 = jnp.zeros((32, 24), jnp.int32)
    p1 = jnp.zeros((32, 24), jnp.int32)
    for s in range(4):
        p0 = jnp.where(t == s, pk_ref[s, 0:1, :], p0)
        p1 = jnp.where(t == s, pk_ref[s, 1:2, :], p1)
    inc = jnp.where((p0 == e) | (p1 == e), 1.0, 0.0)
    before = jnp.where(iota((24, 24), 0) < iota((24, 24), 1), 1.0, 0.0)
    before = dot(inc.astype(BF16), before.astype(BF16))
    ch = jnp.where(before == c.astype(F32), inc, 0.0)
    other = jnp.sum(ch * (p0 + p1 - e).astype(F32), axis=1, keepdims=True)
    n = iota((32, 32), 1) % 16
    e16 = z * 2 + iota((32, 32), 0) // 16
    eo_sc[...] = jnp.where(n == e16, 1.0, 0.0) - jnp.where(n.astype(F32) == other, 1.0, 0.0)
    ch = ch.astype(BF16)
    grow = jnp.where(iota((24, 192), 1) // 8 == iota((24, 192), 0), 1.0, 0.0).astype(BF16)
    wide = dot(ch, grow)
    l8, t_r = iota((32, 192), 1) % 8, (iota((32, 192), 0) // 4) % 4
    chl_sc[...] = jnp.where(l8 == t_r, wide, 0.0).astype(BF16)
    chr_sc[...] = jnp.where(l8 == t_r + 4, wide, 0.0).astype(BF16)
    grow_t = jnp.where(iota((192, 24), 0) // 8 == iota((192, 24), 1), 1.0, 0.0).astype(BF16)
    tall = dot_nt(grow_t, ch)
    r8, t_l = iota((192, 32), 0) % 8, (iota((192, 32), 1) // 4) % 4
    cbl_sc[...] = jnp.where(r8 == t_l, tall, 0.0).astype(BF16)
    cbr_sc[...] = jnp.where(r8 == t_l + 4, tall, 0.0).astype(BF16)
    router = wr_ref[...]
    coarse = router.astype(BF16)
    wr_sc[0:16] = coarse
    wr_sc[16:32] = (router - coarse.astype(F32)).astype(BF16)
    tb_sc[...] = jnp.zeros((8, 128), F32)
    tb_sc[:, 0:32] = jnp.where(iota((8, 32), 0) < 4, rb_ref[0:1, :], rb_ref[1:2, :])

    for load in loads[:4]:
        load.wait()
    x = xb[...].astype(F32)
    root = jnp.sqrt(jnp.mean(x * x, axis=-1, keepdims=True) + EPS)
    scaled = (x / root * ag_ref[...]).astype(BF16)
    i, j = iota((192, 96), 0), iota((192, 96), 1)
    spread = jnp.where(j == (i // 8) * 4 + i % 4, 1.0, 0.0).astype(BF16)
    front = iota((192, 128), 0) % 8 < 4
    q = dot(spread, dot(scaled, wq[...]).astype(BF16))
    q = jnp.where((iota((192, 128), 1) < 64) == front, q, 0.0)
    q_sc[...] = q.reshape(24, 8, 128)
    kn_sc[...] = dot(spread, dot(scaled, wk[...]).astype(BF16)).reshape(24, 8, 128)
    v = dot(spread, dot(scaled, wv[...]).astype(BF16))
    vn_sc[...] = jnp.where(front, v, 0.0).reshape(24, 8, 128)

    loads[4].wait()
    pl.semaphore_wait(barrier, seq_count + head_count - 2)

    row8, lane8 = iota((8, 128), 0), iota((8, 128), 1)
    own = (lane8 < 64) == (row8 < 4)
    wide_row = iota((8, span), 0)
    wide_pos = iota((8, span), 1) + me * span
    table = tb_sc[...]

    def attend(r):
        rel = wide_pos - len_ref[r]
        q8 = q_sc[r].astype(BF16)
        scores = dot_nt(q8, kb[r])
        fresh = dot_nt(q8, kn_sc[r].astype(BF16))
        for t in range(4):
            scores = jnp.where(rel == t, fresh[:, t : t + 1], scores)
        b4 = bb[r]
        b8 = jnp.concatenate([b4, b4], axis=0)
        bias = jnp.concatenate(
            [
                jnp.take_along_axis(
                    table, b8[:, c * 128 : c * 128 + 128], axis=1, mode="promise_in_bounds"
                )
                for c in range(span // 128)
            ],
            axis=1,
        )
        allowed = rel <= wide_row % 4
        scores = jnp.where(allowed, scores + bias, LOW)
        top = jnp.max(scores, axis=1, keepdims=True)
        weights = jnp.where(allowed, jnp.exp(scores - top), 0.0)
        mass = jnp.sum(weights, axis=1, keepdims=True)
        landed = (rel >= 0) & (rel < 4)
        hot = jnp.where(rel == wide_row, 1.0, 0.0).astype(BF16)
        summed = dot(jnp.where(landed, 0.0, weights).astype(BF16), vb[r])
        w_new = dot_nt(weights.astype(BF16), hot)
        summed = summed + dot(w_new.astype(BF16), vn_sc[r].astype(BF16))
        return jnp.where(own, summed, jnp.where(lane8 % 64 < 32, top, mass))

    @pl.loop(0, chunks)
    def _(c):
        cache_load(k_hbm, kb, k_sem, c).wait()
        cache_load(v_hbm, vb, v_sem, c).wait()
        tiles = [attend(c * per + i) for i in range(per)]
        for i in range(per):
            part_sc[c * per + i] = tiles[i]
        for i in range(per):
            r = c * per + i
            target = r + r // 3

            @pl.when(target != me)
            def _():
                slot = (target - me + seq_count) % seq_count
                send(0, part_sc.at[r], in1.at[slot], {"seq": target})

    upper = iota((8, 512), 0) < 4

    def fold(rows):
        return jnp.where(upper, rows[:, :512], rows[:, 512:])

    def pair_mean(values):
        total = jnp.sum(values * values, axis=1, keepdims=True)
        return (total + jnp.concatenate([total[4:8], total[0:4]], axis=0)) / 1024.0

    loads[5].wait()

    @pl.when(owner)
    def _():
        in1[0] = part_sc[mine]
        i, j = iota((8, 96), 0), iota((8, 96), 1)
        pick = jnp.where(j == mine * 4 + i % 4, 1.0, 0.0).astype(BF16)
        states = fold(dot(pick, xb[...]))
        await_bytes(in1.at[pl.ds(0, 31)], recv_sem.at[0])
        part = in1[...]
        r3, l3 = iota((32, 8, 128), 1), iota((32, 8, 128), 2)
        spare = (l3 < 64) != (r3 < 4)
        tops = jnp.max(jnp.where(spare & (l3 % 64 < 32), part, -3e38), axis=2, keepdims=True)
        masses = jnp.max(jnp.where(spare & (l3 % 64 >= 32), part, -3e38), axis=2, keepdims=True)
        lead = jnp.exp(tops - jnp.max(tops, axis=0, keepdims=True))
        mass = jnp.sum(masses * lead, axis=0)
        both = jnp.sum(part * lead, axis=0) / mass
        swapped = jnp.concatenate([both[4:8], both[0:4]], axis=0)
        mixed = jnp.where(own, both, swapped)
        coarse = mixed.astype(BF16)
        fine = (mixed - coarse.astype(F32)).astype(BF16)
        term = fold(dot(coarse, wo[...]) + dot(fine, wo[...])).astype(BF16)
        out2[...] = term
        in2[z] = term

        @pl.loop(1, head_count)
        def _(n):
            send(1, out2, in2.at[z], {"head": (z + n) % head_count})

        await_bytes(in2.at[pl.ds(0, 7)], recv_sem.at[1])
        hidden = states + jnp.sum(in2[...].astype(F32), axis=0)
        hid[...] = hidden
        gain = jnp.where(upper, fg_ref[:, :512], fg_ref[:, 512:])
        normed = (hidden / jnp.sqrt(pair_mean(hidden) + EPS) * gain).astype(BF16)
        out3[...] = normed
        in3[mine] = normed

        @pl.loop(1, seq_count)
        def _(n):
            send(2, out3, in3.at[mine], {"seq": (me + n) % seq_count})

        await_bytes(in3.at[pl.ds(0, 23)], recv_sem.at[2])

    @pl.when(me % 4 == 3)
    def _():
        await_bytes(in3, recv_sem.at[2])

    rows = in3[...].astype(F32).reshape(192, 512).astype(BF16)
    routed = jnp.concatenate([dot(chl_sc[...], rows), dot(chr_sc[...], rows)], axis=1)
    routed = routed.astype(BF16)
    logits = dot_nt(routed, wr_sc[...])
    delta = jnp.sum(logits * eo_sc[...], axis=1, keepdims=True)
    gate = 1.0 / (1.0 + jnp.exp(-delta))
    for load in loads[6:9]:
        load.wait()
    downs = []
    for e in range(2):
        slots = routed[e * 16 : e * 16 + 16]
        gated = jax.nn.gelu(dot_nt(slots, wg[e]), approximate=True)
        units = (gated * dot_nt(slots, wu[e])).astype(BF16)
        downs.append(dot(units, wd[e]))
    down = (jnp.concatenate(downs, axis=0) * gate).astype(BF16)
    spread = dot(cbl_sc[...], down[:, :512]) + dot(cbr_sc[...], down[:, 512:])
    out4[...] = spread.reshape(24, 8, 512).astype(BF16)

    @pl.loop(1, seq_count)
    def _(n):
        target = (me + n) % seq_count

        @pl.when(target % 4 != 3)
        def _():
            request = (target // 4) * 3 + target % 4
            send(3, out4.at[request], in4.at[n], {"seq": target})

    @pl.when(owner)
    def _():
        in4[0] = out4[mine]
        await_bytes(in4.at[pl.ds(0, 31)], recv_sem.at[3])
        mix = jnp.sum(in4[...].astype(F32), axis=0)

        @pl.when(z != home)
        def _():
            out5[...] = mix.astype(BF16)
            send(4, out5, in5.at[z], {"head": home})

        @pl.when(z == home)
        def _():
            in5[z] = mix.astype(BF16)
            await_bytes(in5.at[pl.ds(0, 7)], recv_sem.at[4])
            final = (hid[...] + jnp.sum(in5[...].astype(F32), axis=0)).astype(BF16)
            out6[...] = final
            in6[me % 4] = final

            @pl.loop(1, seq_count)
            def _(n):
                target = {"seq": (me + n) % seq_count}
                send(5, out6, in6.at[me % 4], target, fin_sem.at[me % 4])

    loads[9].wait()
    for k in range(3):

        @pl.when(me != z * 4 + k)
        def _():
            await_bytes(in6.at[k], fin_sem.at[k])

    rows = in6[...].astype(F32)
    total = jnp.sum(rows * rows, axis=2, keepdims=True)
    total = total + jnp.concatenate([total[:, 4:8], total[:, 0:4]], axis=1)
    root = jnp.sqrt(total / 1024.0 + EPS)
    gain = jnp.where(upper, og_ref[:, :512], og_ref[:, 512:])
    scaled = (rows / root * gain[None]).reshape(24, 512).astype(BF16)
    left = dot_nt(scaled, voc[:, :512])
    right = dot_nt(scaled, voc[:, 512:])
    width = voc.shape[0]
    left = left.reshape(3, 8, width)[:, 0:4]
    right = right.reshape(3, 8, width)[:, 4:8]
    best = jnp.max(left + right, axis=2, keepdims=True)
    token = iota((3, 4, 128), 0) * 4 + iota((3, 4, 128), 1)
    place = iota((3, 4, 128), 2) == token
    best = jnp.sum(jnp.sum(jnp.where(place, best, 0.0), axis=0), axis=0, keepdims=True)
    out7[...] = best
    in7[0] = best

    @pl.loop(1, seq_count)
    def _(n):
        send(6, out7, in7.at[n], {"seq": (me + n) % seq_count})

    roots = jnp.sum(jnp.sum(jnp.where(place, root[:, 0:4], 0.0), axis=0), axis=0, keepdims=True)
    halves = [jnp.concatenate([rows[k, 0:4], rows[k, 4:8]], axis=1) for k in range(3)]
    fin_ref[...] = jnp.concatenate(halves, axis=0).astype(BF16)

    @pl.when(owner)
    def _():
        await_bytes(part_sc.at[pl.ds(0, 23)], send_sem.at[0])
        await_bytes(in2.at[pl.ds(0, 7)], send_sem.at[1])
        await_bytes(in4.at[pl.ds(0, 31)], send_sem.at[2])
        await_bytes(out4.at[pl.ds(0, 23)], send_sem.at[3])

        @pl.when(z != home)
        def _():
            await_bytes(out5, send_sem.at[4])

        @pl.when(z == home)
        def _():
            await_bytes(in4.at[pl.ds(0, 31)], send_sem.at[5])

    @pl.when(me % 4 == 3)
    def _():
        await_bytes(part_sc, send_sem.at[0])
        await_bytes(out4, send_sem.at[3])

    await_bytes(in7.at[pl.ds(0, 31)], recv_sem.at[6])
    best = jnp.max(in7[...], axis=0)
    stat_ref[...] = jnp.where(iota((8, 128), 0) == 0, roots, best)
    await_bytes(in7.at[pl.ds(0, 31)], send_sem.at[6])


def deliver_kernel(rows_ref, stat_ref, fin_ref, root_ref, best_ref):
    fin_ref[...] = rows_ref[...]
    root_ref[...] = stat_ref[0, 0:12]
    best_ref[...] = stat_ref[1, 0:12]


def shards(
    new_states,
    lengths,
    cache_keys,
    cache_values,
    buckets,
    attn_gain,
    w_query,
    w_key,
    w_value,
    rel_bias,
    w_out,
    ffn_gain,
    w_router,
    w_gate,
    w_up,
    w_down,
    expert_picks,
    final_gain,
    w_vocab,
):
    whole = pl.BlockSpec(memory_space=pltpu.VMEM)
    smem = pl.BlockSpec(memory_space=pltpu.SMEM)
    anywhere = pl.BlockSpec(memory_space=pl.ANY)
    small = (
        attn_gain[None],
        rel_bias.T,
        jnp.transpose(expert_picks, (0, 2, 1)),
        ffn_gain[None],
        w_router.T,
        final_gain[None],
    )
    large = (
        new_states,
        w_query,
        w_key,
        w_value,
        cache_keys,
        cache_values,
        buckets,
        w_out,
        jnp.transpose(w_gate, (0, 2, 1)),
        jnp.transpose(w_up, (0, 2, 1)),
        w_down,
        w_vocab.T,
    )
    tables = [((32, 192), BF16)] * 2 + [((192, 32), BF16)] * 2 + [((32, 32), F32), ((32, 1024), BF16)]
    staging = [
        ((24, 8, 128), F32),
        ((32, 8, 128), F32),
        ((8, 512), BF16),
        ((8, 8, 512), BF16),
        ((8, 512), BF16),
        ((24, 8, 512), BF16),
        ((24, 8, 512), BF16),
        ((32, 8, 512), BF16),
        ((8, 512), BF16),
        ((8, 8, 512), BF16),
        ((8, 512), BF16),
        ((3, 8, 512), BF16),
        ((1, 128), F32),
        ((32, 1, 128), F32),
        ((8, 512), F32),
    ]
    per = 6
    chunks = cache_keys.shape[0] // per
    rows, stats = pl.pallas_call(
        functools.partial(layer_kernel, per),
        out_shape=(
            jax.ShapeDtypeStruct((12, 1024), BF16),
            jax.ShapeDtypeStruct((8, 128), F32),
        ),
        in_specs=[smem] + [whole] * len(small) + [anywhere] * len(large),
        out_specs=(whole, whole),
        scratch_shapes=[pltpu.VMEM(a.shape, a.dtype) for a in large]
        + [pltpu.VMEM((24, 8, 128), F32)] * 3
        + [pltpu.VMEM((8, 128), F32)]
        + [pltpu.VMEM(s, t) for s, t in tables + staging]
        + [
            pltpu.SemaphoreType.DMA((10,)),
            pltpu.SemaphoreType.DMA((chunks,)),
            pltpu.SemaphoreType.DMA((chunks,)),
            pltpu.SemaphoreType.DMA((7,)),
            pltpu.SemaphoreType.DMA((7,)),
            pltpu.SemaphoreType.DMA((3,)),
        ],
        compiler_params=pltpu.CompilerParams(collective_id=0, has_side_effects=True),
        name="layer",
    )(lengths, *small, *large)
    return pl.pallas_call(
        deliver_kernel,
        out_shape=(
            jax.ShapeDtypeStruct((12, 1024), BF16),
            jax.ShapeDtypeStruct((12,), F32),
            jax.ShapeDtypeStruct((12,), F32),
        ),
        in_specs=[whole] * 2,
        out_specs=(whole,) * 3,
        name="deliver",
    )(rows, stats)


def solution(mesh):
    placed = (
        P(),
        P(),
        P(None, "seq", "head"),
        P(None, "seq", "head"),
        P(None, None, "seq"),
        P(),
        P(None, "head"),
        P(None, "head"),
        P(None, "head"),
        P(None, "head"),
        P("head", None),
        P(),
        P(),
        P("head", None, "seq"),
        P("head", None, "seq"),
        P("head", "seq", None),
        P(),
        P(),
        P(None, "seq"),
    )
    return jax.shard_map(
        shards,
        mesh=mesh,
        in_specs=placed,
        out_specs=(P("head", None), P("head"), P("head")),
        check_vma=False,
    )
```

time: 73.7 us -> 65.1 us (0.88)
  Pallas kernels: 68.9 us -> 64.2 us
  local copies, waits for them, and re-layouts: 3.93 us -> 0 us
    pallas_call x2, Pallas kernels: 68.9 us -> 64.2 us  [the longest x1 62.8 us: shards(): pl.pallas_call(functools.partial(layer_kernel, per), out_shape=(jax.Shape...]
    unnamed x1 -> x0, local copies, waits for them, and re-layouts: 1.37 us -> none
    transpose x1 -> x0, local copies, waits for them, and re-layouts: 1.28 us -> none  [shards(): picks = jnp.transpose(expert_picks, (2, 0, 1)).reshape(8, requests)]
    squeeze x1 -> x0, local copies, waits for them, and re-layouts: 1.27 us -> none  [shards(): return (final, stats[0, :12], stats[1, :12])]
where the time goes in v2:
time: 65.1 us; the launch traced here: 64.9 us
  Pallas kernels  64.2 us (99%)
    pallas_call x1, Pallas kernels, shards(): pl.pallas_call(functools.partial(layer_kernel, per), out_shape=(jax.Shape...  62.8 us
    pallas_call x1, Pallas kernels, shards(): pl.pallas_call(deliver_kernel, out_shape=(jax.ShapeDtypeStruct((12, 1024)...  1.39 us

profile of v2, /device:TPU:1, one launch (start us, length us, event | category | flops | bytes accessed | tf_op | source)
XLA Modules:
  0.0 64.9 jit_solution(3506996842648799721)
XLA Ops:
  0.6 62.8 %layer.1 = (bf16[12,1024]{1,0:T(8,128)(2,1)}, f32[8,128]{1,0:T(8,128)}) custom-call(s32[24]{0:T(128)} %len_ref.1, f32[1,1024]{1,0:T(1,128)} %bitcast.13, f32[2,32]{1,0:T(2,128)} %bitcast.17, s32[4,2,24]{2,1,0:T(2,128)} %bitcast.14, f32[1,1024]{1,0:T(1,128)} %bitcast.15, f32[16,1024]{1,0:T(8,128)} %bitcast.12, f32[1,1024]{1,0:T(1,128)} %bitcast.16, ...), custom_call_target="tpu_custom_call" | custom-call | tf_op jit(solution)/shard_map/layer/pallas_call | solution.py:493
  63.5 1.4 %deliver.1 = (bf16[12,1024]{1,0:T(8,128)(2,1)}, f32[12]{0:T(128)}, f32[12]{0:T(128)}) custom-call(bf16[12,1024]{1,0:T(8,128)(2,1)} %get-tuple-element.5.rows_ref, f32[8,128]{1,0:T(8,128)} %get-tuple-element.6.stat_ref), custom_call_target="tpu_custom_call" | custom-call | tf_op jit(solution)/shard_map/deliver/pallas_call | solution.py:516

commit v3 on v2

--- a/solution.py
+++ b/solution.py
@@ -17,6 +17,14 @@
 HIGH = lax.Precision.HIGHEST
 
 
+def owner_of(request):
+    return (request // 3 + 3 * (request % 3)) % 8 * 4 + request % 3
+
+
+def request_of(position):
+    return (position // 4 + 5 * (position % 4)) % 8 * 3 + position % 4
+
+
 def iota(shape, dim):
     return lax.broadcasted_iota(jnp.int32, shape, dim)
 
@@ -31,13 +39,13 @@
 
 def layer_kernel(
     per,
-    len_ref,
-    ag_ref,
-    rb_ref,
-    pk_ref,
-    fg_ref,
-    wr_ref,
-    og_ref,
+    len_hbm,
+    ag_hbm,
+    rb_hbm,
+    pk_hbm,
+    fg_hbm,
+    wr_hbm,
+    og_hbm,
     x_hbm,
     wq_hbm,
     wk_hbm,
@@ -52,6 +60,13 @@
     voc_hbm,
     fin_ref,
     stat_ref,
+    len_sc,
+    ag_ref,
+    rb_ref,
+    pk_ref,
+    fg_ref,
+    wr_ref,
+    og_ref,
     xb,
     wq,
     wk,
@@ -89,6 +104,7 @@
     out7,
     in7,
     hid,
+    small_sem,
     load_sem,
     k_sem,
     v_sem,
@@ -97,11 +113,20 @@
     fin_sem,
 ):
     seq_count, head_count = 32, 8
+    far = [0, 1, 2, 1]
+    steps = [(dx, dy, dc) for dx in range(4) for dy in range(4) for dc in range(2)]
+    steps = sorted(steps[1:], key=lambda d: (-far[d[0]] - far[d[1]], d))
+    turns = [4, 3, 5, 2, 6, 1, 7]
     me = lax.axis_index("seq")
     z = lax.axis_index("head")
     owner = me % 4 != 3
-    mine = (me // 4) * 3 + me % 4
-    home = me // 4
+    home = (me // 4 + 5 * (me % 4)) % 8
+    mine = home * 3 + me % 4
+    across = [(me // 8 + d) % 4 * 8 for d in range(4)]
+    along = [(me // 2 + d) % 4 * 2 for d in range(4)]
+    side = [(me + d) % 2 for d in range(2)]
+    peers = [(n + 1, across[dx] + along[dy] + side[dc]) for n, (dx, dy, dc) in enumerate(steps)]
+    rings = [(z + n) % head_count for n in turns]
     requests, span = kb.shape[0], kb.shape[1]
     chunks = requests // per
 
@@ -109,6 +134,20 @@
         rows = pl.ds(c * per, per)
         return pltpu.make_async_copy(src.at[rows], dst.at[rows], sem.at[c])
 
+    pairs = [
+        (pk_hbm, pk_ref),
+        (wr_hbm, wr_ref),
+        (rb_hbm, rb_ref),
+        (ag_hbm, ag_ref),
+        (len_hbm, len_sc),
+        (fg_hbm, fg_ref),
+        (og_hbm, og_ref),
+    ]
+    smalls = [
+        pltpu.make_async_copy(src, dst, small_sem.at[n]) for n, (src, dst) in enumerate(pairs)
+    ]
+    for load in smalls:
+        load.start()
     first = [(x_hbm, xb), (wq_hbm, wq), (wk_hbm, wk), (wv_hbm, wv), (b_hbm, bb)]
     later = [(wo_hbm, wo), (wg_hbm, wg), (wu_hbm, wu), (wd_hbm, wd), (voc_hbm, voc)]
     loads = [
@@ -124,17 +163,10 @@
 
     barrier = pltpu.get_barrier_semaphore()
 
-    @pl.loop(1, seq_count)
-    def _(n):
-        pl.semaphore_signal(
-            barrier, inc=1, device_id={"seq": (me + n) % seq_count}, device_id_type=MESH
-        )
-
-    @pl.loop(1, head_count)
-    def _(n):
-        pl.semaphore_signal(
-            barrier, inc=1, device_id={"head": (z + n) % head_count}, device_id_type=MESH
-        )
+    for _, peer in peers:
+        pl.semaphore_signal(barrier, inc=1, device_id={"seq": peer}, device_id_type=MESH)
+    for ring in rings:
+        pl.semaphore_signal(barrier, inc=1, device_id={"head": ring}, device_id_type=MESH)
 
     def send(stage, src, dst, target, sem=None):
         pltpu.make_async_remote_copy(
@@ -148,6 +180,9 @@
 
     def await_bytes(ref, sem):
         pltpu.make_async_copy(ref, ref, sem).wait()
+
+    for load in smalls:
+        load.wait()
 
     i = iota((32, 24), 0)
     e, t, c = z * 2 + i // 16, (i // 4) % 4, i % 4
@@ -202,50 +237,42 @@
 
     row8, lane8 = iota((8, 128), 0), iota((8, 128), 1)
     own = (lane8 < 64) == (row8 < 4)
-    wide_row = iota((8, span), 0)
+    low_lane = lane8 % 64 < 32
     wide_pos = iota((8, span), 1) + me * span
     table = tb_sc[...]
-
-    def attend(r):
-        rel = wide_pos - len_ref[r]
-        q8 = q_sc[r].astype(BF16)
-        scores = dot_nt(q8, kb[r])
-        fresh = dot_nt(q8, kn_sc[r].astype(BF16))
-        for t in range(4):
-            scores = jnp.where(rel == t, fresh[:, t : t + 1], scores)
-        b4 = bb[r]
-        b8 = jnp.concatenate([b4, b4], axis=0)
-        bias = jnp.concatenate(
-            [
-                jnp.take_along_axis(
-                    table, b8[:, c * 128 : c * 128 + 128], axis=1, mode="promise_in_bounds"
-                )
-                for c in range(span // 128)
-            ],
-            axis=1,
-        )
-        allowed = rel <= wide_row % 4
-        scores = jnp.where(allowed, scores + bias, LOW)
-        top = jnp.max(scores, axis=1, keepdims=True)
-        weights = jnp.where(allowed, jnp.exp(scores - top), 0.0)
-        mass = jnp.sum(weights, axis=1, keepdims=True)
-        landed = (rel >= 0) & (rel < 4)
-        hot = jnp.where(rel == wide_row, 1.0, 0.0).astype(BF16)
-        summed = dot(jnp.where(landed, 0.0, weights).astype(BF16), vb[r])
-        w_new = dot_nt(weights.astype(BF16), hot)
-        summed = summed + dot(w_new.astype(BF16), vn_sc[r].astype(BF16))
-        return jnp.where(own, summed, jnp.where(lane8 % 64 < 32, top, mass))
 
     @pl.loop(0, chunks)
     def _(c):
         cache_load(k_hbm, kb, k_sem, c).wait()
         cache_load(v_hbm, vb, v_sem, c).wait()
-        tiles = [attend(c * per + i) for i in range(per)]
-        for i in range(per):
-            part_sc[c * per + i] = tiles[i]
-        for i in range(per):
-            r = c * per + i
-            target = r + r // 3
+        group = [c * per + i for i in range(per)]
+        scores = [dot_nt(q_sc[r].astype(BF16), kb[r]) for r in group]
+        valid = [wide_pos < len_sc[r] for r in group]
+        marks = [bb[r] for r in group]
+        marks = [jnp.concatenate([b, b], axis=0) for b in marks]
+        bias = [
+            jnp.concatenate(
+                [
+                    jnp.take_along_axis(
+                        table, b[:, p : p + 128], axis=1, mode="promise_in_bounds"
+                    )
+                    for p in range(0, span, 128)
+                ],
+                axis=1,
+            )
+            for b in marks
+        ]
+        scores = [jnp.where(ok, a + b, LOW) for ok, a, b in zip(valid, scores, bias)]
+        tops = [jnp.max(a, axis=1, keepdims=True) for a in scores]
+        weights = [
+            jnp.where(ok, jnp.exp(a - top), 0.0) for ok, a, top in zip(valid, scores, tops)
+        ]
+        summed = [dot(w.astype(BF16), vb[r]) for w, r in zip(weights, group)]
+        masses = [jnp.sum(w, axis=1, keepdims=True) for w in weights]
+        for r, top, mass, total in zip(group, tops, masses, summed):
+            part_sc[r] = jnp.where(own, total, jnp.where(low_lane, top, mass))
+        for r in group:
+            target = owner_of(r)
 
             @pl.when(target != me)
             def _():
@@ -266,12 +293,23 @@
     @pl.when(owner)
     def _():
         in1[0] = part_sc[mine]
+        q8 = q_sc[mine].astype(BF16)
+        gap = iota((8, 8), 0) % 4 - iota((8, 8), 1)
+        fresh = dot_nt(q8, kn_sc[mine].astype(BF16))
+        for d in range(4):
+            fresh = fresh + jnp.where(gap == d, table[:, d : d + 1], 0.0)
+        known = gap >= 0
+        top = jnp.max(jnp.where(known, fresh, LOW), axis=1, keepdims=True)
+        weights = jnp.where(known, jnp.exp(fresh - top), 0.0)
+        mass = jnp.sum(weights, axis=1, keepdims=True)
+        total = dot(weights.astype(BF16), vn_sc[mine].astype(BF16))
+        in1[32] = jnp.where(own, total, jnp.where(low_lane, top, mass))
         i, j = iota((8, 96), 0), iota((8, 96), 1)
         pick = jnp.where(j == mine * 4 + i % 4, 1.0, 0.0).astype(BF16)
         states = fold(dot(pick, xb[...]))
         await_bytes(in1.at[pl.ds(0, 31)], recv_sem.at[0])
         part = in1[...]
-        r3, l3 = iota((32, 8, 128), 1), iota((32, 8, 128), 2)
+        r3, l3 = iota((33, 8, 128), 1), iota((33, 8, 128), 2)
         spare = (l3 < 64) != (r3 < 4)
         tops = jnp.max(jnp.where(spare & (l3 % 64 < 32), part, -3e38), axis=2, keepdims=True)
         masses = jnp.max(jnp.where(spare & (l3 % 64 >= 32), part, -3e38), axis=2, keepdims=True)
@@ -286,9 +324,8 @@
         out2[...] = term
         in2[z] = term
 
-        @pl.loop(1, head_count)
-        def _(n):
-            send(1, out2, in2.at[z], {"head": (z + n) % head_count})
+        for ring in rings:
+            send(1, out2, in2.at[z], {"head": ring})
 
         await_bytes(in2.at[pl.ds(0, 7)], recv_sem.at[1])
         hidden = states + jnp.sum(in2[...].astype(F32), axis=0)
@@ -298,9 +335,8 @@
         out3[...] = normed
         in3[mine] = normed
 
-        @pl.loop(1, seq_count)
-        def _(n):
-            send(2, out3, in3.at[mine], {"seq": (me + n) % seq_count})
+        for _, peer in peers:
+            send(2, out3, in3.at[mine], {"seq": peer})
 
         await_bytes(in3.at[pl.ds(0, 23)], recv_sem.at[2])
 
@@ -326,14 +362,11 @@
     spread = dot(cbl_sc[...], down[:, :512]) + dot(cbr_sc[...], down[:, 512:])
     out4[...] = spread.reshape(24, 8, 512).astype(BF16)
 
-    @pl.loop(1, seq_count)
-    def _(n):
-        target = (me + n) % seq_count
-
-        @pl.when(target % 4 != 3)
+    for n, peer in peers:
+
+        @pl.when(peer % 4 != 3)
         def _():
-            request = (target // 4) * 3 + target % 4
-            send(3, out4.at[request], in4.at[n], {"seq": target})
+            send(3, out4.at[request_of(peer)], in4.at[n], {"seq": peer})
 
     @pl.when(owner)
     def _():
@@ -354,15 +387,13 @@
             out6[...] = final
             in6[me % 4] = final
 
-            @pl.loop(1, seq_count)
-            def _(n):
-                target = {"seq": (me + n) % seq_count}
-                send(5, out6, in6.at[me % 4], target, fin_sem.at[me % 4])
+            for _, peer in peers:
+                send(5, out6, in6.at[me % 4], {"seq": peer}, fin_sem.at[me % 4])
 
     loads[9].wait()
     for k in range(3):
 
-        @pl.when(me != z * 4 + k)
+        @pl.when(me != owner_of(z * 3 + k))
         def _():
             await_bytes(in6.at[k], fin_sem.at[k])
 
@@ -384,9 +415,8 @@
     out7[...] = best
     in7[0] = best
 
-    @pl.loop(1, seq_count)
-    def _(n):
-        send(6, out7, in7.at[n], {"seq": (me + n) % seq_count})
+    for n, peer in peers:
+        send(6, out7, in7.at[n], {"seq": peer})
 
     roots = jnp.sum(jnp.sum(jnp.where(place, root[:, 0:4], 0.0), axis=0), axis=0, keepdims=True)
     halves = [jnp.concatenate([rows[k, 0:4], rows[k, 4:8]], axis=1) for k in range(3)]
@@ -446,7 +476,6 @@
     w_vocab,
 ):
     whole = pl.BlockSpec(memory_space=pltpu.VMEM)
-    smem = pl.BlockSpec(memory_space=pltpu.SMEM)
     anywhere = pl.BlockSpec(memory_space=pl.ANY)
     small = (
         attn_gain[None],
@@ -473,7 +502,7 @@
     tables = [((32, 192), BF16)] * 2 + [((192, 32), BF16)] * 2 + [((32, 32), F32), ((32, 1024), BF16)]
     staging = [
         ((24, 8, 128), F32),
-        ((32, 8, 128), F32),
+        ((33, 8, 128), F32),
         ((8, 512), BF16),
         ((8, 8, 512), BF16),
         ((8, 512), BF16),
@@ -496,13 +525,15 @@
             jax.ShapeDtypeStruct((12, 1024), BF16),
             jax.ShapeDtypeStruct((8, 128), F32),
         ),
-        in_specs=[smem] + [whole] * len(small) + [anywhere] * len(large),
+        in_specs=[anywhere] * (1 + len(small) + len(large)),
         out_specs=(whole, whole),
-        scratch_shapes=[pltpu.VMEM(a.shape, a.dtype) for a in large]
+        scratch_shapes=[pltpu.SMEM(lengths.shape, lengths.dtype)]
+        + [pltpu.VMEM(a.shape, a.dtype) for a in small + large]
         + [pltpu.VMEM((24, 8, 128), F32)] * 3
         + [pltpu.VMEM((8, 128), F32)]
         + [pltpu.VMEM(s, t) for s, t in tables + staging]
         + [
+            pltpu.SemaphoreType.DMA((7,)),
             pltpu.SemaphoreType.DMA((10,)),
             pltpu.SemaphoreType.DMA((chunks,)),
             pltpu.SemaphoreType.DMA((chunks,)),

time: 65.1 us -> 52.5 us (0.81)
  Pallas kernels: 64.2 us -> 51.7 us
    pallas_call x1, Pallas kernels: 62.8 us -> 50.3 us  [shards(): pl.pallas_call(functools.partial(layer_kernel, per), out_shape=(jax.Shape...]
where the time goes in v3:
time: 52.5 us; the launch traced here: 52.3 us
  Pallas kernels  51.7 us (98%)
  between operations  0.65 us (1%)
    pallas_call x1, Pallas kernels, shards(): pl.pallas_call(functools.partial(layer_kernel, per), out_shape=(jax.Shape...  50.3 us
    pallas_call x1, Pallas kernels, shards(): pl.pallas_call(deliver_kernel, out_shape=(jax.ShapeDtypeStruct((12, 1024)...  1.39 us

profile of v3, /device:TPU:1, one launch (start us, length us, event | category | flops | bytes accessed | tf_op | source)
XLA Modules:
  0.0 52.3 jit_solution(10147350083042401509)
XLA Ops:
  0.6 50.3 %layer.1 = (bf16[12,1024]{1,0:T(8,128)(2,1)}, f32[8,128]{1,0:T(8,128)}) custom-call(s32[24]{0:T(128)} %len_hbm.1, f32[1,1024]{1,0:T(1,128)} %bitcast.13, f32[2,32]{1,0:T(2,128)} %bitcast.17, s32[4,2,24]{2,1,0:T(2,128)} %bitcast.14, f32[1,1024]{1,0:T(1,128)} %bitcast.15, f32[16,1024]{1,0:T(8,128)} %bitcast.12, f32[1,1024]{1,0:T(1,128)} %bitcast.16, ...), custom_call_target="tpu_custom_call" | custom-call | tf_op jit(solution)/shard_map/layer/pallas_call | solution.py:522
  50.9 1.4 %deliver.1 = (bf16[12,1024]{1,0:T(8,128)(2,1)}, f32[12]{0:T(128)}, f32[12]{0:T(128)}) custom-call(bf16[12,1024]{1,0:T(8,128)(2,1)} %get-tuple-element.5.rows_ref, f32[8,128]{1,0:T(8,128)} %get-tuple-element.6.stat_ref), custom_call_target="tpu_custom_call" | custom-call | tf_op jit(solution)/shard_map/deliver/pallas_call | solution.py:547
